TPU v7x, 512 devices: a whole 4x4x16 slice. The times are simulated.
512 devices in a mesh: rep: 64 (over x, y, z_hi), fsdp: 8 (over z_lo, core).
Axes of the slice: x: 4, y: 4, z: 16 (z_hi: 4, z_lo: 4; z = z_hi * 4 + z_lo), core: 2. Of those that a mesh axis runs over, the one named last changes fastest.
Arguments:
- activations: bfloat16 [64, 4096, 2048], P('rep', 'fsdp'), may hold values from -6 to 6
- cotangent: bfloat16 [64, 4096, 512], P('rep', 'fsdp'), may hold values from -0.079589844 to 0.079589844
- param: bfloat16 [64, 2048, 512], P('rep', 'fsdp'), may hold values from -0.125 to 0.125
- tracker: bfloat16 [64, 2048, 512], P('rep', 'fsdp'), may hold values from -6 to 6
- prev_grad: bfloat16 [64, 2048, 512], P('rep', 'fsdp'), may hold values from -6 to 6
- moment: bfloat16 [64, 2048, 512], P('rep', 'fsdp'), may hold values from -2 to 2
- second: bfloat16 [64, 2048, 512], P('rep', 'fsdp'), may hold values from 0.099609375 to 2
- step: int32 [1], replicated, may hold values from 0 to 4095
Outputs:
- param_out: bfloat16 [64, 2048, 512], P('rep', 'fsdp')
- tracker_out: bfloat16 [64, 2048, 512], P('rep', 'fsdp')
- moment_out: bfloat16 [64, 2048, 512], P('rep', 'fsdp')
- second_out: bfloat16 [64, 2048, 512], P('rep', 'fsdp')
- grad_out: bfloat16 [64, 2048, 512], P('rep', 'fsdp')
Inputs may be any that keep to these rules, and one draw needn't show every extreme that they name: Any step index.
All inputs are finite; a program needn't handle non-finite values.
Results may differ from a plain program's by a relative error of at most 0.014.
Values may be sent and summed in bfloat16 or wider, within the bound.
A program may use at most 64 MiB of HBM per device.

v0:
```python
import functools

import jax
import jax.numpy as jnp
from jax import lax
from jax.sharding import PartitionSpec as P

beta_one = 0.9
beta_two = 0.95
learn_rate = 0.002
epsilon_value = 1e-08


def as_sent(shard):

    def short(part):
        return part.astype(jnp.bfloat16) if part.dtype == jnp.float32 else part

    return jax.tree.map(short, shard)


def passed_along(value, axis, steps):
    count = lax.axis_size(axis)
    pairs = [(source, (source + steps) % count) for source in range(count)]
    return lax.ppermute(value, axis, pairs)


def cut_along(shard, dim, length):
    shape = shard.shape
    pieces = shard.reshape(*shape[:dim], length, shape[dim] // length, *shape[dim + 1 :])
    return jnp.moveaxis(pieces, dim, 0)


def sent_and_summed(shard, axis, dim):
    length = lax.axis_size(axis)
    pieces = lax.all_to_all(cut_along(shard, dim, length), axis, 0, 0, tiled=True)
    return jnp.sum(pieces.astype(jnp.float32), axis=0)


def partner_rows(stacked, bit):
    return jax.tree.map(
        lambda part, own: part.astype(own.dtype),
        passed_along(as_sent(stacked), "rep", 1 << bit),
        stacked,
    )


def mix_with_partner(param, tracker, step):
    levels = lax.axis_size("rep").bit_length() - 1
    branches = [functools.partial(partner_rows, bit=bit) for bit in range(levels)]
    index = step[0] % levels
    stacked = jnp.stack([param[0], tracker[0]], axis=0)
    far_rows = lax.switch(index, branches, stacked)
    mixed_param = 0.5 * (param[0].astype(jnp.float32) + far_rows[0].astype(jnp.float32))
    mixed_tracker = 0.5 * (tracker[0].astype(jnp.float32) + far_rows[1].astype(jnp.float32))
    return (mixed_param, mixed_tracker)


def gradient(activations, cotangent):
    tokens_here = activations[0]
    cotan_here = cotangent[0]
    return sent_and_summed(
        lax.dot_general(
            tokens_here, cotan_here, (((0,), (0,)), ((), ())), preferred_element_type=jnp.float32
        ).astype(jnp.bfloat16),
        "fsdp",
        0,
    )


def body(activations, cotangent, param, tracker, prev_grad, moment, second, step):
    grad = gradient(activations, cotangent)
    mixed_param, mixed_tracker = mix_with_partner(param, tracker, step)
    new_tracker = mixed_tracker + grad - prev_grad[0].astype(jnp.float32)
    new_moment = beta_one * moment[0].astype(jnp.float32) + (1.0 - beta_one) * new_tracker
    new_second = (
        beta_two * second[0].astype(jnp.float32) + (1.0 - beta_two) * new_tracker * new_tracker
    )
    count = (step[0] + 1).astype(jnp.float32)
    correct_one = 1.0 - jnp.power(jnp.float32(beta_one), count)
    correct_two = 1.0 - jnp.power(jnp.float32(beta_two), count)
    update = new_moment / correct_one / (jnp.sqrt(new_second / correct_two) + epsilon_value)
    param_out = (mixed_param - learn_rate * update).astype(jnp.bfloat16)
    return (
        param_out[None],
        new_tracker.astype(jnp.bfloat16)[None],
        new_moment.astype(jnp.bfloat16)[None],
        new_second.astype(jnp.bfloat16)[None],
        grad.astype(jnp.bfloat16)[None],
    )


def solution(mesh):
    in_specs = (
        P("rep", "fsdp", None),
        P("rep", "fsdp", None),
        P("rep", "fsdp", None),
        P("rep", "fsdp", None),
        P("rep", "fsdp", None),
        P("rep", "fsdp", None),
        P("rep", "fsdp", None),
        P(),
    )
    out_specs = (
        P("rep", "fsdp", None),
        P("rep", "fsdp", None),
        P("rep", "fsdp", None),
        P("rep", "fsdp", None),
        P("rep", "fsdp", None),
    )
    return jax.shard_map(body, mesh=mesh, in_specs=in_specs, out_specs=out_specs, check_vma=False)
```

profile of v0, /device:TPU:1, one launch (start us, length us, event | category | flops | bytes accessed | tf_op | source)
XLA Modules:
  0.0 72.2 jit_solution(10746571448121030336)
XLA Ops:
  0.6 0.0 copy-start
  0.6 1.6 %copy-done = bf16[1,512,2048]{2,1,0:T(8,128)(2,1)S(1)} copy-done((bf16[1,512,2048]{2,1,0:T(8,128)(2,1)S(1)}, bf16[1,512,2048]{2,1,0:T(8,128)(2,1)}, u32[]{:S(2)}) %copy-start) | copy-done | bytes 2097176
  2.2 3.7 %convolution_convert_fusion = bf16[2048,512]{1,0:T(8,128)(2,1)} fusion(bf16[1,512,2048]{2,1,0:T(8,128)(2,1)S(1)} %copy-done, bf16[1,512,512]{2,1,0:T(8,128)(2,1)} %param.15), kind=kOutput, calls=%fused_computation.1 | convolution fusion | flops 1074790400 | bytes 4718592 | tf_op jit(solution)/shard_map/dot_general | solution.py:63
  5.9 0.0 copy-start.2
  5.9 0.0 copy-start.3
  5.9 11.2 %all-to-all-start = ((bf16[8,256,512]{2,1,0:T(8,128)(2,1)}), bf16[8,256,512]{2,1,0:T(8,128)(2,1)}, u32[]{:S(2)}, u32[]{:S(2)}) async-start(bf16[8,256,512]{2,1,0:T(8,128)(2,1)} %bitcast.16), calls=%async_computation | async-start | bytes 4194304 | tf_op jit(solution)/shard_map/all_to_all | solution.py:36
  17.8 0.0 copy-done.2
  17.8 0.0 copy-done.3
  17.9 0.0 copy-start.1
  17.9 0.0 copy-start.4
  17.9 0.1 pad_maximum_fusion
  17.9 16.7 %conditional.1 = (bf16[2,256,512]{2,1,0:T(8,128)(2,1)}) conditional(s32[]{:T(128)} %clamp.3, bf16[2,256,512]{2,1,0:T(8,128)(2,1)S(1)} %pad_maximum_fusion, bf16[2,256,512]{2,1,0:T(8,128)(2,1)S(1)} %pad_maximum_fusion, bf16[2,256,512]{2,1,0:T(8,128)(2,1)S(1)} %pad_maximum_fusion, ...), branch_computations={%region_0.0_spmd, %region_1.2_spmd, %region_2.3_spmd, %region_3.4_... | conditional | bytes 2097200 | solution.py:53
  18.0 2.1 %collective-permute-start.4 = (bf16[2,256,512]{2,1,0:T(8,128)(2,1)S(1)}, bf16[2,256,512]{2,1,0:T(8,128)(2,1)}, u32[]{:S(2)}, u32[]{:S(2)}) collective-permute-start(bf16[2,256,512]{2,1,0:T(8,128)(2,1)S(1)} %param.4), channel_id=1, source_target_pairs={{0,128},{8,136},{16,144},{24,152},{32,160},{40,168},{48,176},{56,1... | collective-permute-start | bytes 1572872 | tf_op jit(solution)/shard_map/cond/branch_4_fun/ppermute | solution.py:25
  20.0 14.6 %collective-permute-done.4 = bf16[2,256,512]{2,1,0:T(8,128)(2,1)} collective-permute-done((bf16[2,256,512]{2,1,0:T(8,128)(2,1)S(1)}, bf16[2,256,512]{2,1,0:T(8,128)(2,1)}, u32[]{:S(2)}, u32[]{:S(2)}) %collective-permute-start.4) | collective-permute-done | bytes 524320 | tf_op jit(solution)/shard_map/cond/branch_4_fun/ppermute | solution.py:25
  34.7 30.6 %all-to-all-done = bf16[8,256,512]{2,1,0:T(8,128)(2,1)} async-done(((bf16[8,256,512]{2,1,0:T(8,128)(2,1)}), bf16[8,256,512]{2,1,0:T(8,128)(2,1)}, u32[]{:S(2)}, u32[]{:S(2)}) %all-to-all-start) | async-done | bytes 2097184 | tf_op jit(solution)/shard_map/all_to_all | solution.py:36
  65.3 1.9 %convert_reduce_fusion = f32[256,512]{1,0:T(8,128)S(1)} fusion(bf16[8,256,512]{2,1,0:T(8,128)(2,1)} %all-to-all-done), kind=kLoop, calls=%fused_computation | loop fusion | flops 1966080 | bytes 2621440 | tf_op jit(solution)/shard_map/reduce_sum | solution.py:37
  67.2 0.0 copy-start.5
  67.2 0.7 %bitcast_convert_fusion = bf16[1,256,512]{2,1,0:T(8,128)(2,1)} fusion(f32[256,512]{1,0:T(8,128)S(1)} %convert_reduce_fusion), kind=kLoop, calls=%fused_computation.6 | loop fusion | flops 131072 | bytes 786432 | tf_op jit(solution)/shard_map/convert_element_type | solution.py:89
  68.0 0.0 copy-done.1
  68.0 0.0 copy-done.4
  68.0 1.9 %fusion.5 = (bf16[1,256,512]{2,1,0:T(8,128)(2,1)}, f32[1,256,512]{2,1,0:T(8,128)S(1)}) fusion(bf16[1,256,512]{2,1,0:T(8,128)(2,1)S(1)} %copy-done.1, bf16[1,256,512]{2,1,0:T(8,128)(2,1)S(1)} %copy-done.4, f32[256,512]{1,0:T(8,128)S(1)} %convert_reduce_fusion, bf16[2,256,512]{2,1,0:T(8,128)(2,1)} %get-tuple-element.23, bf16[1,256,512]{2,1,0:T(8,128)(2,1)S(1)} %copy-done.2), kind=kLoop, calls=%fused_computation.13 | loop fusion | flops 1703936 | bytes 2359296 | tf_op jit(solution)/shard_map/convert_element_type | solution.py:88
  69.9 0.0 copy-done.5
  69.9 2.3 %fusion.4 = (bf16[1,256,512]{2,1,0:T(8,128)(2,1)}, bf16[1,256,512]{2,1,0:T(8,128)(2,1)}, bf16[1,256,512]{2,1,0:T(8,128)(2,1)}) fusion(f32[1,256,512]{2,1,0:T(8,128)S(1)} %get-tuple-element.19, bf16[1,256,512]{2,1,0:T(8,128)(2,1)S(1)} %copy-done.5, f32[]{:T(128)} %bitcast.6, bf16[1,256,512]{2,1,0:T(8,128)(2,1)S(1)} %copy-done.1, f32[]{:T(128)} %bitcast.5, ...), kind=kLoop, calls=%fused_computation.12 | loop fusion | flops 2883584 | bytes 2359304 | tf_op jit(solution)/shard_map/convert_element_type | solution.py:87
Async XLA Ops:
  0.6 1.6 %copy-start = (bf16[1,512,2048]{2,1,0:T(8,128)(2,1)S(1)}, bf16[1,512,2048]{2,1,0:T(8,128)(2,1)}, u32[]{:S(2)}) copy-start(bf16[1,512,2048]{2,1,0:T(8,128)(2,1)} %param.14) | copy-start | bytes 6291460
  5.9 12.0 %copy-start.2 = (bf16[1,256,512]{2,1,0:T(8,128)(2,1)S(1)}, bf16[1,256,512]{2,1,0:T(8,128)(2,1)}, u32[]{:S(2)}) copy-start(bf16[1,256,512]{2,1,0:T(8,128)(2,1)} %param.17) | copy-start | bytes 786436
  5.9 12.0 %copy-start.3 = (bf16[1,256,512]{2,1,0:T(8,128)(2,1)S(1)}, bf16[1,256,512]{2,1,0:T(8,128)(2,1)}, u32[]{:S(2)}) copy-start(bf16[1,256,512]{2,1,0:T(8,128)(2,1)} %param.16) | copy-start | bytes 786436
  5.9 59.4 %all-to-all-start = ((bf16[8,256,512]{2,1,0:T(8,128)(2,1)}), bf16[8,256,512]{2,1,0:T(8,128)(2,1)}, u32[]{:S(2)}, u32[]{:S(2)}) async-start(bf16[8,256,512]{2,1,0:T(8,128)(2,1)} %bitcast.16), calls=%async_computation | async-start | bytes 4194304 | tf_op jit(solution)/shard_map/all_to_all | solution.py:36
  17.9 50.1 %copy-start.1 = (bf16[1,256,512]{2,1,0:T(8,128)(2,1)S(1)}, bf16[1,256,512]{2,1,0:T(8,128)(2,1)}, u32[]{:S(2)}) copy-start(bf16[1,256,512]{2,1,0:T(8,128)(2,1)} %param.20) | copy-start | bytes 786436
  17.9 50.1 %copy-start.4 = (bf16[1,256,512]{2,1,0:T(8,128)(2,1)S(1)}, bf16[1,256,512]{2,1,0:T(8,128)(2,1)}, u32[]{:S(2)}) copy-start(bf16[1,256,512]{2,1,0:T(8,128)(2,1)} %param.18) | copy-start | bytes 786436
  18.0 16.7 %collective-permute-start.4 = (bf16[2,256,512]{2,1,0:T(8,128)(2,1)S(1)}, bf16[2,256,512]{2,1,0:T(8,128)(2,1)}, u32[]{:S(2)}, u32[]{:S(2)}) collective-permute-start(bf16[2,256,512]{2,1,0:T(8,128)(2,1)S(1)} %param.4), channel_id=1, source_target_pairs={{0,128},{8,136},{16,144},{24,152},{32,160},{40,168},{48,176},{56,1... | collective-permute-start | bytes 1572872 | tf_op jit(solution)/shard_map/cond/branch_4_fun/ppermute | solution.py:25
  67.2 2.6 %copy-start.5 = (bf16[1,256,512]{2,1,0:T(8,128)(2,1)S(1)}, bf16[1,256,512]{2,1,0:T(8,128)(2,1)}, u32[]{:S(2)}) copy-start(bf16[1,256,512]{2,1,0:T(8,128)(2,1)} %param.19) | copy-start | bytes 786436
where the time goes:
time: 72.6 us; the launch traced here: 72.2 us
  waiting for transfers between devices  45.3 us (62%)
  starting transfers between devices  13.2 us (18%)
  other arithmetic  6.95 us (10%)
  matrix products  3.66 us (5%)
  local copies, waits for them, and re-layouts  1.62 us (2%)
  between operations  1.45 us (2%)
    all_to_all x1, waiting for transfers between devices, sent_and_summed(): lax.all_to_all(cut_along(shard, dim, length), axis, 0, 0, tiled=True)  30.6 us
    ppermute x1, waiting for transfers between devices, passed_along(): return lax.ppermute(value, axis, pairs)  14.6 us
    all_to_all x1, starting transfers between devices, sent_and_summed(): lax.all_to_all(cut_along(shard, dim, length), axis, 0, 0, tiled=True)  11.2 us
    dot_general x1, matrix products, gradient(): lax.dot_general(tokens_here, cotan_here, (((0,), (0,)), ((), ())), prefer...  3.66 us
    convert_element_type x1, other arithmetic, body(): new_moment.astype(jnp.bfloat16)[None]  2.33 us
    ppermute x1, starting transfers between devices, passed_along(): return lax.ppermute(value, axis, pairs)  2.05 us
    reduce_sum x1, other arithmetic, sent_and_summed(): return jnp.sum(pieces.astype(jnp.float32), axis=0)  1.94 us
    convert_element_type x1, other arithmetic, body(): new_second.astype(jnp.bfloat16)[None]  1.89 us
  transfers between devices with their start and end apart: 2, of which 2 were waited for; matrix products, arithmetic and copies ran while one was open for 0% of the time, Pallas kernels for 0%

commit v1 on v0

v1 whole, which is shorter than its diff:
```python
import functools

import jax
import jax.numpy as jnp
from jax import lax
from jax.experimental import pallas as pl
from jax.experimental.pallas import tpu as pltpu
from jax.sharding import PartitionSpec as P

beta_one = 0.9
beta_two = 0.95
learn_rate = 0.002
epsilon_value = 1e-08

MESH = pl.DeviceIdType.MESH
CHIPS = 4
PIECES = 4
HALVES = 2
F32 = jnp.float32
BF16 = jnp.bfloat16


def kernel(
    shift,
    scal_ref,
    act_hbm,
    cot_hbm,
    param_hbm,
    tracker_hbm,
    prev_hbm,
    moment_hbm,
    second_hbm,
    param_out,
    tracker_out,
    moment_out,
    second_out,
    grad_out,
    act,
    cot,
    acc,
    mate_send,
    mate_recv,
    line_send,
    line_recv,
    far,
    state,
    result,
    act_sem,
    cot_sem,
    state_sem,
    result_sem,
    mate_ssem,
    mate_rsem,
    line_ssem,
    line_rsem,
    far_ssem,
    far_rsem,
):
    reps = lax.axis_size("rep")
    rep = lax.axis_index("rep")
    col = lax.axis_index("fsdp")
    z = col // 2
    core = col % 2
    mate = (rep, col + 1 - 2 * core)
    far_to = (lax.rem(rep + shift, reps), col)
    far_from = (lax.rem(rep + reps - shift, reps), col)
    rows = param_hbm.shape[0]
    piece = rows // PIECES
    half = rows // HALVES
    last = CHIPS - 1

    upper = z // 2
    inner = (z + upper) % 2
    code = 27 + 72 * inner

    def dest(k):
        plain = (code // (4**k)) % 4 if isinstance(k, int) else lax.shift_right_logical(code, 2 * k) % 4
        return plain + upper * (last - 2 * plain)

    barrier = pltpu.get_barrier_semaphore()
    pl.semaphore_signal(barrier, inc=1, device_id=mate, device_id_type=MESH)

    @pl.when(z > 0)
    def _():
        pl.semaphore_signal(barrier, inc=1, device_id=(rep, col - 2), device_id_type=MESH)

    @pl.when(z < last)
    def _():
        pl.semaphore_signal(barrier, inc=1, device_id=(rep, col + 2), device_id_type=MESH)

    pl.semaphore_signal(barrier, inc=1, device_id=far_from, device_id_type=MESH)
    pl.semaphore_signal(barrier, inc=1, device_id=far_to, device_id_type=MESH)

    def act_load(k):
        start = pl.multiple_of(dest(k) * (2 * rows), 2 * rows)
        return pltpu.make_async_copy(
            act_hbm.at[:, pl.ds(start, 2 * rows)], act.at[k], act_sem.at[k]
        )

    cot_load = pltpu.make_async_copy(cot_hbm, cot, cot_sem)
    cot_load.start()
    act_load(0).start()
    act_load(1).start()
    act_load(2).start()
    act_load(3).start()
    state_loads = [
        pltpu.make_async_copy(ref, state.at[n], state_sem.at[n])
        for n, ref in enumerate((param_hbm, tracker_hbm, prev_hbm, moment_hbm, second_hbm))
    ]
    for load in state_loads:
        load.start()

    far_copies = [
        pltpu.make_async_remote_copy(
            src_ref=ref,
            dst_ref=far.at[n],
            send_sem=far_ssem.at[n],
            recv_sem=far_rsem.at[n],
            device_id=far_to,
            device_id_type=MESH,
        )
        for n, ref in enumerate((param_hbm, tracker_hbm))
    ]

    def mate_copy(k, h):
        part = pl.ds(h * half, half)
        return pltpu.make_async_remote_copy(
            src_ref=mate_send.at[k, part],
            dst_ref=mate_recv.at[k, part],
            send_sem=mate_ssem.at[k, h],
            recv_sem=mate_rsem.at[k, h],
            device_id=mate,
            device_id_type=MESH,
        )

    def term(k, which):
        columns = pl.ds(pl.multiple_of(which * rows, rows), rows)
        return lax.dot_general(
            act[k, :, columns], cot[...], (((0,), (0,)), ((), ())), preferred_element_type=F32
        )

    def line_copy(k, p):
        d = dest(k)
        way = jnp.where(d > z, 1, -1)
        slot = jnp.where((d == z + way) & (way < 0), CHIPS, d)
        part = pl.ds(p * piece, piece)
        return pltpu.make_async_remote_copy(
            src_ref=line_send.at[k, part],
            dst_ref=line_recv.at[slot, part],
            send_sem=line_ssem.at[k, p],
            recv_sem=line_rsem.at[slot, p],
            device_id=(rep, col + 2 * way),
            device_id_type=MESH,
        )

    def arrival(slot, p):
        part = pl.ds(p * piece, piece)
        return pltpu.make_async_remote_copy(
            src_ref=line_send.at[0, part],
            dst_ref=line_recv.at[slot, part],
            send_sem=line_ssem.at[0, p],
            recv_sem=line_rsem.at[slot, p],
            device_id=mate,
            device_id_type=MESH,
        )

    def wait_barrier():
        ends = jnp.where(z > 0, 1, 0) + jnp.where(z < last, 1, 0)
        pl.semaphore_wait(barrier, 3 + ends)

    def compute(k):
        act_load(k).wait()
        mate_send[k] = term(k, 1 - core).astype(BF16)

        @pl.when(k == 0)
        def _():
            wait_barrier()

        for h in range(HALVES):
            mate_copy(k, h).start()

        @pl.when(k == 0)
        def _():
            for copy in far_copies:
                copy.start()

        acc[k] = term(k, core)

    def pass_on(k):
        d = dest(k)
        way = jnp.where(d > z, 1, -1)
        behind = z - way
        fed = (behind >= 0) & (behind <= last)
        for p in range(PIECES):
            part = pl.ds(p * piece, piece)
            if p % (PIECES // HALVES) == 0:
                mate_copy(k, p // (PIECES // HALVES)).wait_recv()
            own = acc[k, part] + mate_recv[k, part].astype(F32)

            @pl.when(fed)
            def _():
                arrival(d, p).wait_recv()
                line_send[k, part] = (own + line_recv[d, part].astype(F32)).astype(BF16)

            @pl.when(jnp.logical_not(fed))
            def _():
                line_send[k, part] = own.astype(BF16)

            line_copy(k, p).start()

    cot_load.wait()

    def step(i, carry):
        @pl.when(i < CHIPS)
        def _():
            compute(i)

        @pl.when((i >= 1) & (i < CHIPS))
        def _():
            pass_on(i - 1)

        return carry

    lax.fori_loop(0, CHIPS, step, 0)

    for load in state_loads:
        load.wait()
    for copy in far_copies:
        copy.wait_recv()
    scale_one = scal_ref[0]
    scale_two = scal_ref[1]

    def result_copy(n, ref, p):
        part = pl.ds(p * piece, piece)
        return pltpu.make_async_copy(result.at[n, part], ref.at[part], result_sem.at[n, p])

    outs = (param_out, tracker_out, moment_out, second_out, grad_out)

    def finish(p, carry):
        part = pl.ds(pl.multiple_of(p * piece, piece), piece)

        @pl.when(p % (PIECES // HALVES) == 0)
        def _():
            mate_copy(last, p // (PIECES // HALVES)).wait_recv()

        acc[last, part] += mate_recv[last, part].astype(F32)

        @pl.when(z > 0)
        def _():
            arrival(z, p).wait_recv()
            acc[last, part] += line_recv[z, part].astype(F32)

        @pl.when(z < last)
        def _():
            arrival(CHIPS, p).wait_recv()
            acc[last, part] += line_recv[CHIPS, part].astype(F32)

        grad = acc[last, part]
        mixed_param = 0.5 * (state[0, part].astype(F32) + far[0, part].astype(F32))
        mixed_tracker = 0.5 * (state[1, part].astype(F32) + far[1, part].astype(F32))
        new_tracker = mixed_tracker + grad - state[2, part].astype(F32)
        new_moment = beta_one * state[3, part].astype(F32) + (1.0 - beta_one) * new_tracker
        new_second = (
            beta_two * state[4, part].astype(F32) + (1.0 - beta_two) * new_tracker * new_tracker
        )
        update = (new_moment * scale_one) / (jnp.sqrt(new_second * scale_two) + epsilon_value)
        values = (mixed_param - learn_rate * update, new_tracker, new_moment, new_second, grad)
        for n, value in enumerate(values):
            result[n, part] = value.astype(BF16)
        for n, ref in enumerate(outs):
            result_copy(n, ref, p).start()
        return carry

    lax.fori_loop(0, PIECES, finish, 0)

    for n, ref in enumerate(outs):
        for p in range(PIECES):
            result_copy(n, ref, p).wait()
    for copy in far_copies:
        copy.wait_send()
    for k in range(CHIPS):
        for h in range(HALVES):
            mate_copy(k, h).wait_send()
    for k in range(CHIPS - 1):
        for p in range(PIECES):
            line_copy(k, p).wait_send()


def step_at(index, scal, act, cot, param, tracker, prev, moment, second):
    tokens, width = act.shape
    rows, columns = param.shape
    out = jax.ShapeDtypeStruct((rows, columns), BF16)
    anywhere = pl.BlockSpec(memory_space=pl.ANY)
    dma = pltpu.SemaphoreType.DMA
    return pl.pallas_call(
        functools.partial(kernel, 1 << index),
        out_shape=[out] * 5,
        in_specs=[pl.BlockSpec(memory_space=pltpu.SMEM)] + [anywhere] * 7,
        out_specs=[anywhere] * 5,
        scratch_shapes=[
            pltpu.VMEM((CHIPS, tokens, 2 * rows), BF16),
            pltpu.VMEM((tokens, columns), BF16),
            pltpu.VMEM((CHIPS, rows, columns), F32),
            pltpu.VMEM((CHIPS, rows, columns), BF16),
            pltpu.VMEM((CHIPS, rows, columns), BF16),
            pltpu.VMEM((CHIPS - 1, rows, columns), BF16),
            pltpu.VMEM((CHIPS + 1, rows, columns), BF16),
            pltpu.VMEM((2, rows, columns), BF16),
            pltpu.VMEM((5, rows, columns), BF16),
            pltpu.VMEM((5, rows, columns), BF16),
            dma((CHIPS,)),
            dma,
            dma((5,)),
            dma((5, PIECES)),
            dma((CHIPS, HALVES)),
            dma((CHIPS, HALVES)),
            dma((CHIPS - 1, PIECES)),
            dma((CHIPS + 1, PIECES)),
            dma((2,)),
            dma((2,)),
        ],
        compiler_params=pltpu.CompilerParams(
            collective_id=index, has_side_effects=True, vmem_limit_bytes=40 * 2**20
        ),
        name=f"step_{index}",
    )(scal, act, cot, param, tracker, prev, moment, second)


def settle_kernel(*refs):
    ins, outs, bufs, isem, osem = refs[:5], refs[5:10], refs[10], refs[11], refs[12]
    loads = [pltpu.make_async_copy(ref, bufs.at[n], isem.at[n]) for n, ref in enumerate(ins)]
    stores = [pltpu.make_async_copy(bufs.at[n], ref, osem.at[n]) for n, ref in enumerate(outs)]
    for load in loads:
        load.start()
    for load, store in zip(loads, stores):
        load.wait()
        store.start()
    for store in stores:
        store.wait()


def settle(values):
    rows, columns = values[0].shape
    anywhere = pl.BlockSpec(memory_space=pl.ANY)
    return pl.pallas_call(
        settle_kernel,
        out_shape=[jax.ShapeDtypeStruct((rows, columns), BF16)] * 5,
        in_specs=[anywhere] * 5,
        out_specs=[anywhere] * 5,
        scratch_shapes=[
            pltpu.VMEM((5, rows, columns), BF16),
            pltpu.SemaphoreType.DMA((5,)),
            pltpu.SemaphoreType.DMA((5,)),
        ],
        compiler_params=pltpu.CompilerParams(vmem_limit_bytes=4 * 2**20),
        name="settle",
    )(*values)


def body(activations, cotangent, param, tracker, prev_grad, moment, second, step):
    levels = lax.axis_size("rep").bit_length() - 1
    count = (step[0] + 1).astype(F32)
    correct_one = 1.0 - jnp.power(jnp.float32(beta_one), count)
    correct_two = 1.0 - jnp.power(jnp.float32(beta_two), count)
    scal = jnp.stack([1.0 / correct_one, 1.0 / correct_two])
    values = lax.switch(
        step[0] % levels,
        [functools.partial(step_at, index) for index in range(levels)],
        scal,
        activations[0],
        cotangent[0],
        param[0],
        tracker[0],
        prev_grad[0],
        moment[0],
        second[0],
    )
    return tuple(value[None] for value in settle(values))


def solution(mesh):
    spread = P("rep", "fsdp", None)
    return jax.shard_map(
        body,
        mesh=mesh,
        in_specs=(spread,) * 7 + (P(),),
        out_specs=(spread,) * 5,
        check_vma=False,
    )
```

time: 72.6 us -> 32.2 us (0.44)
  the two profiles are of different devices: /device:TPU:1 before, /device:TPU:32 now
where the time goes in v1:
time: 32.2 us; the launch traced here: 32.1 us
  Pallas kernels  30.6 us (95%)
  between operations  1.47 us (5%)
    pallas_call x1, Pallas kernels, step_at(): pl.pallas_call(functools.partial(kernel, 1 << index), out_shape=[out] * 5...  29.3 us
    pallas_call x1, Pallas kernels, settle(): pl.pallas_call(settle_kernel, out_shape=[jax.ShapeDtypeStruct((rows, colu...  1.23 us

profile of v1, /device:TPU:32, one launch (start us, length us, event | category | flops | bytes accessed | tf_op | source)
XLA Modules:
  0.0 32.1 jit_solution(10381709045746449220)
XLA Ops:
  1.5 0.1 pad_maximum_fusion
  1.5 29.3 %conditional.1 = ((bf16[256,512]{1,0:T(8,128)(2,1)S(1)}, bf16[256,512]{1,0:T(8,128)(2,1)S(1)}, bf16[256,512]{1,0:T(8,128)(2,1)S(1)}, bf16[256,512]{1,0:T(8,128)(2,1)S(1)}, bf16[256,512]{1,0:T(8,128)(2,1)S(1)})) conditional(s32[]{:T(128)} %clamp.3, (f32[2]{0:T(128)S(1)}, bf16[512,2048]{1,0:T(8,128)(2,1)}, ...), branch_computations={%region_0.1_spmd, %region_1.2_spmd, %region_2.3_spmd, %region_3.4_... | conditional | bytes 8 | solution.py:366
  1.5 29.3 %step_2.1 = (bf16[256,512]{1,0:T(8,128)(2,1)S(1)}, bf16[256,512]{1,0:T(8,128)(2,1)S(1)}, bf16[256,512]{1,0:T(8,128)(2,1)S(1)}, bf16[256,512]{1,0:T(8,128)(2,1)S(1)}, bf16[256,512]{1,0:T(8,128)(2,1)S(1)}) custom-call(f32[2]{0:T(128)S(1)} %get-tuple-element.112.scal_ref, bf16[512,2048]{1,0:T(8,128)(2,1)} %get-tuple-element.113.act_hbm, ...), custom_call_target="tpu_custom_call" | custom-call | tf_op jit(solution)/shard_map/cond/branch_2_fun/step_2/pallas_call | solution.py:295
  30.9 1.2 %settle.1 = (bf16[256,512]{1,0:T(8,128)(2,1)}, bf16[256,512]{1,0:T(8,128)(2,1)}, bf16[256,512]{1,0:T(8,128)(2,1)}, bf16[256,512]{1,0:T(8,128)(2,1)}, bf16[256,512]{1,0:T(8,128)(2,1)}) custom-call(bf16[256,512]{1,0:T(8,128)(2,1)S(1)} %get-tuple-element.159.refs_0_, bf16[256,512]{1,0:T(8,128)(2,1)S(1)} %get-tuple-element.160.refs_1_, ...), custom_call_target="tpu_custom_call" | custom-call | tf_op jit(solution)/shard_map/settle/pallas_call | solution.py:345
